TPU v7x, 32 devices: a whole 2x2x4 slice. The times are simulated.
32 devices in a mesh: row: 4 (over z), col: 8 (over y, x, core).
Axes of the slice: x: 2, y: 2, z: 4, core: 2. Of those that a mesh axis runs over, the one named last changes fastest.
Arguments:
- block_cells: float32 [352, 5, 16, 256], P(('row', 'col')), may hold values from -0.6 to 1.4, as said below
- slot_blocks: int32 [32, 11], replicated, may hold values from -1 to 191, as said below
Outputs:
- new_cells: float32 [224, 5, 16, 256], P(('row', 'col'))
Inputs may be any that keep to these rules, and one draw needn't show every extreme that they name: `slot_blocks`: row r * 8 + c lists the blocks held by device (r, c): block ids first, in slot order, then -1. Block b belongs to column group b // 24, and every block of column group c is held by exactly one device of that column group. Each device holds 1 to 11 blocks, the devices of a column group hold 24 blocks together, and in every column group one device holds 11 blocks and one holds 1. `block_cells`: fields 0 and 4 (density, pressure) lie in 0.7 to 1.4 and fields 1 to 3 (velocity) in -0.6 to 0.6. Slots marked -1 in slot_blocks hold values that no output depends on.
All inputs are finite; a program needn't handle non-finite values.
Results may differ from a plain program's by a relative error of at most 0.0001.
Values sent between devices are 32-bit elements; how exact they have to be, the bound alone decides.
A program may use at most 64 MiB of HBM per device.

v0:
```python
import jax
import jax.numpy as jnp
from jax import lax
from jax.sharding import PartitionSpec as P

BLK_MEAN = 6
OUT = 7
heat_ratio = 1.4
time_step = 0.12
thermal_leading_multiplier = 0.2
thermal_power_law_index = 0.7


def swapped(array, axis, apart):
    return lax.ppermute(array, axis, [(i, i ^ 1 << apart) for i in range(lax.axis_size(axis))])


def from_behind(block, axis, distance):
    devices = range(lax.axis_size(axis))
    route = [((i - distance) % len(devices), i) for i in devices]
    return lax.ppermute(block, axis, route)


def rebalance_table(anchors, counts):
    row_count, columns, slot_width = anchors.shape
    slot_ids = jnp.arange(slot_width, dtype=jnp.int32)
    row_ids = jnp.arange(row_count, dtype=jnp.int32)
    for section_bit in range(row_count.bit_length() - 1):
        partner = row_ids ^ 1 << section_bit
        other_anchors = anchors[partner]
        other_counts = counts[partner]
        sending = jnp.maximum(counts - other_counts, 0) // 2
        taking = jnp.maximum(other_counts - counts, 0) // 2
        keeping = (counts - sending)[:, :, None]
        anchor_slot = other_counts[:, :, None] - taking[:, :, None] + slot_ids - keeping
        pulled = jnp.take_along_axis(
            other_anchors, jnp.clip(anchor_slot, 0, slot_width - 1), axis=2
        )
        anchors = jnp.where(
            slot_ids < keeping,
            anchors,
            jnp.where(slot_ids < keeping + taking[:, :, None], pulled, -1),
        )
        counts = counts - sending + taking
    return (anchors, counts)


def to_conserved(primitive):
    matter_per_volume = primitive[0]
    velocity = primitive[1:4]
    fluid_static_stress = primitive[4]
    energy = fluid_static_stress / (heat_ratio - 1.0) + 0.5 * matter_per_volume * jnp.sum(
        velocity * velocity, axis=0
    )
    return jnp.concatenate(
        [matter_per_volume[None], matter_per_volume[None] * velocity, energy[None]], axis=0
    )


def to_primitive(conserved):
    matter_per_volume = conserved[0]
    velocity = conserved[1:4] / matter_per_volume
    fluid_static_stress = (heat_ratio - 1.0) * (
        conserved[4] - 0.5 * matter_per_volume * jnp.sum(velocity * velocity, axis=0)
    )
    return jnp.concatenate([matter_per_volume[None], velocity, fluid_static_stress[None]], axis=0)


def cell_terms(conserved, normal):
    matter_per_volume = conserved[0]
    momentum = conserved[1:4]
    velocity = momentum / matter_per_volume
    fluid_static_stress = (heat_ratio - 1.0) * (
        conserved[4] - 0.5 * matter_per_volume * jnp.sum(velocity * velocity, axis=0)
    )
    perpendicular_flow_rate = velocity[normal]
    moment_flux = momentum * perpendicular_flow_rate
    moment_flux = moment_flux.at[normal].add(fluid_static_stress)
    face_transport_amounts = jnp.concatenate(
        [
            momentum[normal][None],
            moment_flux,
            ((conserved[4] + fluid_static_stress) * perpendicular_flow_rate)[None],
        ],
        axis=0,
    )
    sound_signal_rate = jnp.sqrt(heat_ratio * fluid_static_stress / matter_per_volume)
    fluid_thermal_state = fluid_static_stress / matter_per_volume
    thermal_diffusivity_factor = thermal_leading_multiplier * jnp.power(
        fluid_thermal_state, thermal_power_law_index
    )
    return (
        face_transport_amounts,
        jnp.abs(perpendicular_flow_rate) + sound_signal_rate,
        fluid_thermal_state,
        thermal_diffusivity_factor,
        fluid_static_stress,
    )


def face_flux(lower_cons, lower_data, upper_cons, upper_data):
    wave_speed = jnp.maximum(lower_data[1], upper_data[1])
    face_transport_amounts = 0.5 * (lower_data[0] + upper_data[0]) - 0.5 * wave_speed[None] * (
        upper_cons - lower_cons
    )
    heat_flow = 0.5 * (lower_data[3] + upper_data[3]) * (upper_data[2] - lower_data[2])
    return face_transport_amounts.at[4].add(-heat_flow)


def wall_flux(fluid_static_stress, normal):
    nothing = jnp.zeros_like(fluid_static_stress)
    members = [nothing, nothing, nothing, nothing, nothing]
    members[normal + 1] = fluid_static_stress
    return jnp.stack(members, axis=0)


def cut_rows(tree, first_index, last_index):
    return jax.tree.map(lambda member: member[..., first_index:last_index, :], tree)


def cut_flat(tree, first_index, last_index):
    return jax.tree.map(lambda member: member[..., first_index:last_index], tree)


def block_tendency(conserved, low_x, high_x, low_y, high_y):
    block_edge = conserved.shape[1]
    flat_size = conserved.shape[2]
    padded_x = jnp.concatenate([low_x, conserved, high_x], axis=1)
    cell_data = cell_terms(padded_x, 0)
    face_transport_amounts = face_flux(
        padded_x[:, :-1],
        cut_rows(cell_data, 0, block_edge + 1),
        padded_x[:, 1:],
        cut_rows(cell_data, 1, block_edge + 2),
    )
    change_x = face_transport_amounts[:, 1:] - face_transport_amounts[:, :-1]
    padded_y = jnp.concatenate([low_y, conserved, high_y], axis=2)
    cell_data = cell_terms(padded_y, 1)
    reach_end = flat_size + block_edge
    face_transport_amounts = face_flux(
        padded_y[..., :reach_end],
        cut_flat(cell_data, 0, reach_end),
        padded_y[..., block_edge:],
        cut_flat(cell_data, block_edge, reach_end + block_edge),
    )
    change_y = face_transport_amounts[..., block_edge:] - face_transport_amounts[..., :flat_size]
    cell_data = cell_terms(conserved, 2)
    interior = face_flux(
        conserved[..., :-1],
        cut_flat(cell_data, 0, flat_size - 1),
        conserved[..., 1:],
        cut_flat(cell_data, 1, flat_size),
    )
    nothing = jnp.zeros_like(interior[..., :1])
    wall_values = wall_flux(cell_data[4], 2)
    height = jnp.arange(flat_size, dtype=jnp.int32) % block_edge
    upper_face = jnp.where(
        height == block_edge - 1, wall_values, jnp.concatenate([interior, nothing], axis=-1)
    )
    lower_face = jnp.where(height == 0, wall_values, jnp.concatenate([nothing, interior], axis=-1))
    change_z = upper_face - lower_face
    return -(change_x + change_y + change_z)


def body(block_cells, slot_blocks):
    row_count = lax.axis_size("row")
    columns = lax.axis_size("col")
    my_row = lax.axis_index("row")
    my_col = lax.axis_index("col")
    slot_width = slot_blocks.shape[1]
    per_group = BLK_MEAN * row_count
    send_slots = BLK_MEAN - 1
    block_edge = block_cells.shape[2]
    flat_size = block_cells.shape[3]
    every_slot = slot_blocks.reshape(-1)
    occupied = slot_blocks >= 0
    counts = jnp.sum(occupied.astype(jnp.int32), axis=1).reshape(row_count, columns)
    device_ids = jnp.arange(row_count * columns, dtype=jnp.int32)[:, None]
    anchors = jnp.where(
        occupied, device_ids * slot_width + jnp.arange(slot_width, dtype=jnp.int32)[None, :], -1
    )
    anchors = anchors.reshape(row_count, columns, slot_width)
    final_anchors, final_counts = rebalance_table(anchors, counts)
    final_anchors = final_anchors[:, :, :OUT]
    my_anchors = final_anchors[my_row, my_col]
    row_ids = jnp.arange(row_count, dtype=jnp.int32)
    holding = block_cells
    counts_now = counts
    slot_ids = jnp.arange(slot_width, dtype=jnp.int32)
    for section_bit in range(row_count.bit_length() - 1):
        partner = row_ids ^ 1 << section_bit
        other_counts = counts_now[partner]
        sending = jnp.maximum(counts_now - other_counts, 0) // 2
        taking = jnp.maximum(other_counts - counts_now, 0) // 2
        keeping = counts_now[my_row, my_col] - sending[my_row, my_col]
        send_from = jnp.clip(keeping + jnp.arange(send_slots, dtype=jnp.int32), 0, slot_width - 1)
        outgoing = jnp.take(holding, send_from, axis=0)
        incoming = swapped(outgoing, "row", section_bit)
        candidates = jnp.concatenate([holding, incoming], axis=0)
        chosen = jnp.where(
            slot_ids < keeping,
            slot_ids,
            slot_width + jnp.clip(slot_ids - keeping, 0, send_slots - 1),
        )
        holding = jnp.take(candidates, chosen, axis=0)
        counts_now = counts_now - sending + taking
    holding = holding[:OUT]
    active = my_anchors >= 0
    benign = jnp.array([1.0, 0.0, 0.0, 0.0, 1.0], jnp.float32)[None, :, None, None]
    holding = jnp.where(active[:, None, None, None], holding, benign)
    initial = jax.vmap(to_conserved)(holding)
    my_blocks = every_slot[jnp.maximum(my_anchors, 0)]
    along_y = jnp.clip(my_blocks - my_col * per_group, 0, per_group - 1)
    below_col = (my_col - 1) % columns
    above_col = (my_col + 1) % columns

    def located(column, wanted):
        anchors_here = final_anchors[:, column].reshape(-1)
        blocks_here = jnp.where(anchors_here >= 0, every_slot[jnp.maximum(anchors_here, 0)], -1)
        return jnp.argmax(blocks_here[None, :] == wanted[:, None], axis=1)

    from_x_low = located(below_col, below_col * per_group + along_y)
    from_y_low = located(below_col, below_col * per_group + (along_y - 1) % per_group)
    from_x_high = located(above_col, above_col * per_group + along_y)
    from_y_high = located(above_col, above_col * per_group + (along_y + 1) % per_group)

    def section_rate(current):
        highs = jnp.stack(
            [
                current[:, :, block_edge - 1, :],
                current[:, :, :, flat_size - block_edge :].reshape(OUT, 5, flat_size),
            ],
            axis=1,
        )
        lows = jnp.stack(
            [current[:, :, 0, :], current[:, :, :, :block_edge].reshape(OUT, 5, flat_size)], axis=1
        )
        passed_highs = from_behind(highs, "col", 1)
        passed_lows = from_behind(lows, "col", -1)
        from_below, from_above = (
            lax.all_gather(passed_highs, "row", axis=0, tiled=True),
            lax.all_gather(passed_lows, "row", axis=0, tiled=True),
        )
        low_x = from_below[from_x_low, 0][:, :, None, :]
        low_y = from_below[from_y_low, 1].reshape(OUT, 5, block_edge, block_edge)
        high_x = from_above[from_x_high, 0][:, :, None, :]
        high_y = from_above[from_y_high, 1].reshape(OUT, 5, block_edge, block_edge)
        return jax.vmap(block_tendency)(current, low_x, high_x, low_y, high_y)

    first_section = initial + time_step * section_rate(initial)
    second_section = 0.75 * initial + 0.25 * (
        first_section + time_step * section_rate(first_section)
    )
    third_section = 1.0 / 3.0 * initial + 2.0 / 3.0 * (
        second_section + time_step * section_rate(second_section)
    )
    result = jax.vmap(to_primitive)(third_section)
    return jnp.where(active[:, None, None, None], result, jnp.zeros_like(result)).astype(
        jnp.float32
    )


def solution(mesh):
    in_specs = (P(("row", "col"), None, None, None), P())
    out_specs = P(("row", "col"), None, None, None)
    return jax.shard_map(body, mesh=mesh, in_specs=in_specs, out_specs=out_specs, check_vma=False)
```

profile of v0, /device:TPU:0, one launch (start us, length us, event | category | flops | bytes accessed | tf_op | source)
XLA Modules:
  0.0 179.7 jit_solution(13251556273873494992)
XLA Ops:
  0.0 0.8 copy.142
  1.7 0.6 dynamic_slice.24
  2.3 0.7 dynamic_slice.26
  7.2 1.7 gather_fusion.21
  9.0 3.1 %collective-permute-start = (f32[5,5,16,256]{3,2,1,0:T(8,128)S(1)}, f32[5,5,16,256]{3,2,1,0:T(8,128)S(1)}, u32[]{:S(2)}, u32[]{:S(2)}) collective-permute-start(f32[5,5,16,256]{3,2,1,0:T(8,128)S(1)} %broadcast_select_fusion.2), channel_id=1, source_target_pairs={{0,8},{8,0},{16,24},{24,16},{1,9},{9,1},{17,25},{25,17},{2,10},{10... | collective-permute-start | bytes 1228808 | tf_op jit(solution)/shard_map/ppermute | solution.py:15
  13.4 4.0 %gather_fusion.19 = s32[352]{0:T(512)S(1)} fusion(s32[4,8,11]{2,1,0:T(8,128)S(1)} %gather_fusion.2, s32[352]{0:T(512)S(1)} %reshape.1164), kind=kCustom, calls=%fused_computation.clone | custom fusion | bytes 7040 | tf_op jit(solution)/shard_map/jit(take_along_axis)/gather | solution.py:36
  18.2 4.0 %gather_fusion.20 = s32[352]{0:T(512)S(1)} fusion(s32[4,8,11]{2,1,0:T(8,128)S(1)} %gather_fusion.3, s32[352]{0:T(512)S(1)} %reshape.1169), kind=kCustom, calls=%fused_computation.3.clone | custom fusion | bytes 7040 | tf_op jit(solution)/shard_map/jit(take_along_axis)/gather | solution.py:36
  22.9 0.7 gather_fusion.7
  23.6 0.7 gather_fusion.4
  24.3 0.6 gather_fusion.5
  25.0 0.7 iota_reduce_fusion.2
  25.7 0.7 iota_reduce_fusion
  26.5 0.7 iota_reduce_fusion.3
  27.2 0.7 iota_reduce_fusion.1
  28.0 0.6 gather_fusion.22
  29.5 2.7 %collective-permute-start.1 = (f32[5,5,16,256]{3,2,1,0:T(8,128)S(1)}, f32[5,5,16,256]{3,2,1,0:T(8,128)S(1)}, u32[]{:S(2)}, u32[]{:S(2)}) collective-permute-start(f32[5,5,16,256]{3,2,1,0:T(8,128)S(1)} %broadcast_select_fusion.1), channel_id=1, source_target_pairs={{0,16},{8,24},{16,0},{24,8},{1,17},{9,25},{17,1},{25,9},{2,18},{10... | collective-permute-start | bytes 1228808 | tf_op jit(solution)/shard_map/ppermute | solution.py:15
  32.1 17.8 %collective-permute-done.1 = f32[5,5,16,256]{3,2,1,0:T(8,128)S(1)} collective-permute-done((f32[5,5,16,256]{3,2,1,0:T(8,128)S(1)}, f32[5,5,16,256]{3,2,1,0:T(8,128)S(1)}, u32[]{:S(2)}, u32[]{:S(2)}) %collective-permute-start.1) | collective-permute-done | bytes 409632 | tf_op jit(solution)/shard_map/ppermute | solution.py:15
  50.1 0.6 gather_fusion.24
  52.2 2.2 %collective-permute-start.3 = (f32[7,2,5,256]{3,1,2,0:T(2,128)S(1)}, f32[7,2,5,256]{3,1,2,0:T(2,128)S(1)}, u32[]{:S(2)}, u32[]{:S(2)}) collective-permute-start(f32[7,2,5,256]{3,1,2,0:T(2,128)S(1)} %pad_maximum_fusion.29), channel_id=1, source_target_pairs={{1,0},{2,1},{3,2},{4,3},{5,4},{6,5},{7,6},{0,7},{9,8},{10,9},{11,1... | collective-permute-start | bytes 215048 | tf_op jit(solution)/shard_map/ppermute | solution.py:21
  55.1 4.1 %collective-permute-done.2 = f32[7,2,5,256]{3,1,2,0:T(2,128)S(1)} collective-permute-done((f32[7,2,5,256]{3,1,2,0:T(2,128)S(1)}, f32[7,2,5,256]{3,1,2,0:T(2,128)S(1)}, u32[]{:S(2)}, u32[]{:S(2)}) %collective-permute-start.2) | collective-permute-done | bytes 71712 | tf_op jit(solution)/shard_map/ppermute | solution.py:21
  59.2 14.6 %all_gather.18 = f32[28,2,5,256]{3,1,2,0:T(2,128)S(1)} all-gather(f32[7,2,5,256]{3,1,2,0:T(2,128)S(1)} %collective-permute-done.2), channel_id=1, replica_groups=mesh['row'=4,'col'=8] {'row'}, dimensions={0}, use_global_device_ids=true | all-gather | bytes 358400 | tf_op jit(solution)/shard_map/all_gather | solution.py:241
  74.4 13.9 %all_gather.19 = f32[28,2,5,256]{3,1,2,0:T(2,128)S(1)} all-gather(f32[7,2,5,256]{3,1,2,0:T(2,128)S(1)} %collective-permute-done.3), channel_id=1, replica_groups=mesh['row'=4,'col'=8] {'row'}, dimensions={0}, use_global_device_ids=true | all-gather | bytes 358400 | tf_op jit(solution)/shard_map/all_gather | solution.py:242
  90.4 1.6 gather_fusion.8
  96.8 0.7 collective-permute-start.4
  98.1 3.6 %collective-permute-done.4 = f32[7,2,5,256]{3,1,2,0:T(2,128)S(1)} collective-permute-done((f32[7,2,5,256]{3,1,2,0:T(2,128)S(1)}, f32[7,2,5,256]{3,1,2,0:T(2,128)S(1)}, u32[]{:S(2)}, u32[]{:S(2)}) %collective-permute-start.4) | collective-permute-done | bytes 71712 | tf_op jit(solution)/shard_map/ppermute | solution.py:21
  101.7 14.2 %all_gather.20 = f32[28,2,5,256]{3,1,2,0:T(2,128)S(1)} all-gather(f32[7,2,5,256]{3,1,2,0:T(2,128)S(1)} %collective-permute-done.4), channel_id=1, replica_groups=mesh['row'=4,'col'=8] {'row'}, dimensions={0}, use_global_device_ids=true | all-gather | bytes 358400 | tf_op jit(solution)/shard_map/all_gather | solution.py:241
  117.1 14.4 %all_gather.21 = f32[28,2,5,256]{3,1,2,0:T(2,128)S(1)} all-gather(f32[7,2,5,256]{3,1,2,0:T(2,128)S(1)} %collective-permute-done.5), channel_id=1, replica_groups=mesh['row'=4,'col'=8] {'row'}, dimensions={0}, use_global_device_ids=true | all-gather | bytes 358400 | tf_op jit(solution)/shard_map/all_gather | solution.py:242
  139.6 3.6 %collective-permute-done.6 = f32[7,2,5,256]{3,1,2,0:T(2,128)S(1)} collective-permute-done((f32[7,2,5,256]{3,1,2,0:T(2,128)S(1)}, f32[7,2,5,256]{3,1,2,0:T(2,128)S(1)}, u32[]{:S(2)}, u32[]{:S(2)}) %collective-permute-start.6) | collective-permute-done | bytes 71712 | tf_op jit(solution)/shard_map/ppermute | solution.py:21
  143.2 14.1 %all_gather.22 = f32[28,2,5,256]{3,1,2,0:T(2,128)S(1)} all-gather(f32[7,2,5,256]{3,1,2,0:T(2,128)S(1)} %collective-permute-done.6), channel_id=1, replica_groups=mesh['row'=4,'col'=8] {'row'}, dimensions={0}, use_global_device_ids=true | all-gather | bytes 358400 | tf_op jit(solution)/shard_map/all_gather | solution.py:241
  158.6 14.4 %all_gather.23 = f32[28,2,5,256]{3,1,2,0:T(2,128)S(1)} all-gather(f32[7,2,5,256]{3,1,2,0:T(2,128)S(1)} %collective-permute-done.7), channel_id=1, replica_groups=mesh['row'=4,'col'=8] {'row'}, dimensions={0}, use_global_device_ids=true | all-gather | bytes 358400 | tf_op jit(solution)/shard_map/all_gather | solution.py:242
  178.0 0.6 fusion.47
  178.9 0.8 copy.184
  (257 shorter events, 31.5 us)
Async XLA Ops:
  9.0 18.9 %collective-permute-start = (f32[5,5,16,256]{3,2,1,0:T(8,128)S(1)}, f32[5,5,16,256]{3,2,1,0:T(8,128)S(1)}, u32[]{:S(2)}, u32[]{:S(2)}) collective-permute-start(f32[5,5,16,256]{3,2,1,0:T(8,128)S(1)} %broadcast_select_fusion.2), channel_id=1, source_target_pairs={{0,8},{8,0},{16,24},{24,16},{1,9},{9,1},{17,25},{25,17},{2,10},{10... | collective-permute-start | bytes 1228808 | tf_op jit(solution)/shard_map/ppermute | solution.py:15
  22.2 5.7 %copy-start = (f32[11,5,16,256]{3,2,1,0:T(8,128)S(1)}, f32[11,5,16,256]{3,2,1,0:T(8,128)}, u32[]{:S(2)}) copy-start(f32[11,5,16,256]{3,2,1,0:T(8,128)} %param.45) | copy-start | bytes 2703364
  29.5 20.5 %collective-permute-start.1 = (f32[5,5,16,256]{3,2,1,0:T(8,128)S(1)}, f32[5,5,16,256]{3,2,1,0:T(8,128)S(1)}, u32[]{:S(2)}, u32[]{:S(2)}) collective-permute-start(f32[5,5,16,256]{3,2,1,0:T(8,128)S(1)} %broadcast_select_fusion.1), channel_id=1, source_target_pairs={{0,16},{8,24},{16,0},{24,8},{1,17},{9,25},{17,1},{25,9},{2,18},{10... | collective-permute-start | bytes 1228808 | tf_op jit(solution)/shard_map/ppermute | solution.py:15
  50.1 0.7 copy-start.2
  52.2 22.2 %collective-permute-start.3 = (f32[7,2,5,256]{3,1,2,0:T(2,128)S(1)}, f32[7,2,5,256]{3,1,2,0:T(2,128)S(1)}, u32[]{:S(2)}, u32[]{:S(2)}) collective-permute-start(f32[7,2,5,256]{3,1,2,0:T(2,128)S(1)} %pad_maximum_fusion.29), channel_id=1, source_target_pairs={{1,0},{2,1},{3,2},{4,3},{5,4},{6,5},{7,6},{0,7},{9,8},{10,9},{11,1... | collective-permute-start | bytes 215048 | tf_op jit(solution)/shard_map/ppermute | solution.py:21
  54.5 4.7 %collective-permute-start.2 = (f32[7,2,5,256]{3,1,2,0:T(2,128)S(1)}, f32[7,2,5,256]{3,1,2,0:T(2,128)S(1)}, u32[]{:S(2)}, u32[]{:S(2)}) collective-permute-start(f32[7,2,5,256]{3,1,2,0:T(2,128)S(1)} %pad_maximum_fusion.28), channel_id=1, source_target_pairs={{7,0},{0,1},{1,2},{2,3},{3,4},{4,5},{5,6},{6,7},{15,8},{8,9},{9,10... | collective-permute-start | bytes 215048 | tf_op jit(solution)/shard_map/ppermute | solution.py:21
  88.4 0.8 copy-start.1
  96.6 20.5 %collective-permute-start.5 = (f32[7,2,5,256]{3,1,2,0:T(2,128)S(1)}, f32[7,2,5,256]{3,1,2,0:T(2,128)S(1)}, u32[]{:S(2)}, u32[]{:S(2)}) collective-permute-start(f32[7,2,5,256]{3,1,2,0:T(2,128)S(1)} %pad_maximum_fusion.31), channel_id=1, source_target_pairs={{1,0},{2,1},{3,2},{4,3},{5,4},{6,5},{7,6},{0,7},{9,8},{10,9},{11,1... | collective-permute-start | bytes 215048 | tf_op jit(solution)/shard_map/ppermute | solution.py:21
  96.8 4.9 %collective-permute-start.4 = (f32[7,2,5,256]{3,1,2,0:T(2,128)S(1)}, f32[7,2,5,256]{3,1,2,0:T(2,128)S(1)}, u32[]{:S(2)}, u32[]{:S(2)}) collective-permute-start(f32[7,2,5,256]{3,1,2,0:T(2,128)S(1)} %pad_maximum_fusion.30), channel_id=1, source_target_pairs={{7,0},{0,1},{1,2},{2,3},{3,4},{4,5},{5,6},{6,7},{15,8},{8,9},{9,10... | collective-permute-start | bytes 215048 | tf_op jit(solution)/shard_map/ppermute | solution.py:21
  138.3 20.2 %collective-permute-start.7 = (f32[7,2,5,256]{3,1,2,0:T(2,128)S(1)}, f32[7,2,5,256]{3,1,2,0:T(2,128)S(1)}, u32[]{:S(2)}, u32[]{:S(2)}) collective-permute-start(f32[7,2,5,256]{3,1,2,0:T(2,128)S(1)} %pad_maximum_fusion.33), channel_id=1, source_target_pairs={{1,0},{2,1},{3,2},{4,3},{5,4},{6,5},{7,6},{0,7},{9,8},{10,9},{11,1... | collective-permute-start | bytes 215048 | tf_op jit(solution)/shard_map/ppermute | solution.py:21
  138.5 4.7 %collective-permute-start.6 = (f32[7,2,5,256]{3,1,2,0:T(2,128)S(1)}, f32[7,2,5,256]{3,1,2,0:T(2,128)S(1)}, u32[]{:S(2)}, u32[]{:S(2)}) collective-permute-start(f32[7,2,5,256]{3,1,2,0:T(2,128)S(1)} %pad_maximum_fusion.32), channel_id=1, source_target_pairs={{7,0},{0,1},{1,2},{2,3},{3,4},{4,5},{5,6},{6,7},{15,8},{8,9},{9,10... | collective-permute-start | bytes 215048 | tf_op jit(solution)/shard_map/ppermute | solution.py:21
where the time goes:
time: 180 us
  blocking collectives  85.5 us (48%)
  local copies, waits for them, and re-layouts  32.5 us (18%)
  waiting for transfers between devices  29.1 us (16%)
  other arithmetic  19.2 us (11%)
  starting transfers between devices  9.39 us (5%)
  between operations  3.94 us (2%)
    all_gather x3, blocking collectives, section_rate(): lax.all_gather(passed_highs, 'row', axis=0, tiled=True)  42.9 us
    all_gather x3, blocking collectives, section_rate(): lax.all_gather(passed_lows, 'row', axis=0, tiled=True)  42.7 us
    ppermute x2, waiting for transfers between devices, swapped(): lax.ppermute(array, axis, [(i, i ^ 1 << apart) for i in range(lax.axis_si...  17.8 us
    ppermute x6, waiting for transfers between devices, from_behind(): return lax.ppermute(block, axis, route)  11.3 us
    gather x6, local copies, waits for them, and re-layouts, rebalance_table(): jnp.take_along_axis(other_anchors, jnp.clip(anchor_slot, 0, slot_width -...  8.44 us
    ppermute x2, starting transfers between devices, swapped(): lax.ppermute(array, axis, [(i, i ^ 1 << apart) for i in range(lax.axis_si...  5.78 us
    sub x9, other arithmetic, face_flux(): 0.5 * (lower_data[0] + upper_data[0])  3.63 us
    ppermute x6, starting transfers between devices, from_behind(): return lax.ppermute(block, axis, route)  3.61 us
  transfers between devices with their start and end apart: 8, of which 4 were waited for; matrix products, arithmetic and copies ran while one was open for 11% of the time, Pallas kernels for 0%

commit v1 on v0

--- a/solution.py
+++ b/solution.py
@@ -238,7 +238,10 @@
         passed_highs = from_behind(highs, "col", 1)
         passed_lows = from_behind(lows, "col", -1)
         from_below, from_above = (
-            lax.all_gather(passed_highs, "row", axis=0, tiled=True),
+            jnp.concatenate(
+                lax.all_to_all(jnp.stack([passed_highs] * lax.axis_size("row")), "row", 0, 0),
+                axis=0,
+            ),
             lax.all_gather(passed_lows, "row", axis=0, tiled=True),
         )
         low_x = from_below[from_x_low, 0][:, :, None, :]

time: 180 us -> 159 us (0.88)
  blocking collectives: 85.5 us -> 47.3 us
  starting transfers between devices: 9.39 us -> 19.7 us
  local copies, waits for them, and re-layouts: 32.5 us -> 36.7 us
  waiting for transfers between devices: 29.1 us -> 31 us
    all_gather x3 -> x0, blocking collectives: 42.9 us -> none  [section_rate(): lax.all_gather(passed_highs, 'row', axis=0, tiled=True)]
    all_to_all x0 -> x3, starting transfers between devices: none -> 10.5 us  [section_rate(): lax.all_to_all(jnp.stack([passed_highs] * lax.axis_size('row')), 'row', 0...]
    all_gather x3, blocking collectives: 42.7 us -> 47.3 us  [section_rate(): lax.all_gather(passed_lows, 'row', axis=0, tiled=True)]
    another operation x2 -> x5, local copies, waits for them, and re-layouts: 0.01 us -> 2.37 us  [the longest x3 2.36 us: section_rate(): jnp.stack([passed_highs] * lax.axis_size('row'))]
    ppermute x6, waiting for transfers between devices: 11.3 us -> 13.2 us  [from_behind(): return lax.ppermute(block, axis, route)]
  transfers between devices with their start and end apart: 8 -> 11, of which waited for: 4 -> 4; matrix products, arithmetic and copies ran while one was open for 11% -> 16% of each run, Pallas kernels for 0% -> 0%
where the time goes in v1:
time: 159 us; the launch traced here: 158 us
  blocking collectives  47.3 us (30%)
  local copies, waits for them, and re-layouts  36.7 us (23%)
  waiting for transfers between devices  31 us (19%)
  starting transfers between devices  19.7 us (12%)
  other arithmetic  19.3 us (12%)
  between operations  4.41 us (3%)
    all_gather x3, blocking collectives, section_rate(): lax.all_gather(passed_lows, 'row', axis=0, tiled=True)  47.3 us
    ppermute x2, waiting for transfers between devices, swapped(): lax.ppermute(array, axis, [(i, i ^ 1 << apart) for i in range(lax.axis_si...  17.8 us
    ppermute x6, waiting for transfers between devices, from_behind(): return lax.ppermute(block, axis, route)  13.2 us
    all_to_all x3, starting transfers between devices, section_rate(): lax.all_to_all(jnp.stack([passed_highs] * lax.axis_size('row')), 'row', 0...  10.5 us
    gather x6, local copies, waits for them, and re-layouts, rebalance_table(): jnp.take_along_axis(other_anchors, jnp.clip(anchor_slot, 0, slot_width -...  8.44 us
    ppermute x2, starting transfers between devices, swapped(): lax.ppermute(array, axis, [(i, i ^ 1 << apart) for i in range(lax.axis_si...  5.78 us
    sub x9, other arithmetic, face_flux(): 0.5 * (lower_data[0] + upper_data[0])  3.66 us
    ppermute x6, starting transfers between devices, from_behind(): return lax.ppermute(block, axis, route)  3.43 us
  transfers between devices with their start and end apart: 11, of which 4 were waited for; matrix products, arithmetic and copies ran while one was open for 16% of the time, Pallas kernels for 0%

profile of v1, /device:TPU:0, one launch (start us, length us, event | category | flops | bytes accessed | tf_op | source)
XLA Modules:
  0.0 158.4 jit_solution(4212053589018604607)
XLA Ops:
  0.0 0.8 copy.142
  2.9 0.7 dynamic_slice.25
  5.5 0.7 dynamic_slice.27
  7.5 1.7 %gather_fusion.21 = f32[5,5,16,256]{3,2,1,0:T(8,128)S(1)} fusion(f32[11,5,16,256]{3,2,1,0:T(8,128)} %param.45, s32[1024]{0:T(1024)S(1)} %pad_clamp_fusion.6), kind=kCustom, calls=%fused_computation.1.clone | custom fusion | bytes 819220 | tf_op jit(solution)/shard_map/jit(_take)/gather | solution.py:197
  9.4 3.1 %collective-permute-start = (f32[5,5,16,256]{3,2,1,0:T(8,128)S(1)}, f32[5,5,16,256]{3,2,1,0:T(8,128)S(1)}, u32[]{:S(2)}, u32[]{:S(2)}) collective-permute-start(f32[5,5,16,256]{3,2,1,0:T(8,128)S(1)} %broadcast_select_fusion.2), channel_id=1, source_target_pairs={{0,8},{8,0},{16,24},{24,16},{1,9},{9,1},{17,25},{25,17},{2,10},{10... | collective-permute-start | bytes 1228808 | tf_op jit(solution)/shard_map/ppermute | solution.py:15
  13.7 4.0 %gather_fusion.19 = s32[352]{0:T(512)S(1)} fusion(s32[4,8,11]{2,1,0:T(8,128)S(1)} %gather_fusion.2, s32[352]{0:T(512)S(1)} %reshape.1182), kind=kCustom, calls=%fused_computation.clone | custom fusion | bytes 7040 | tf_op jit(solution)/shard_map/jit(take_along_axis)/gather | solution.py:36
  18.5 4.0 %gather_fusion.20 = s32[352]{0:T(512)S(1)} fusion(s32[4,8,11]{2,1,0:T(8,128)S(1)} %gather_fusion.3, s32[352]{0:T(512)S(1)} %reshape.1187), kind=kCustom, calls=%fused_computation.3.clone | custom fusion | bytes 7040 | tf_op jit(solution)/shard_map/jit(take_along_axis)/gather | solution.py:36
  23.3 0.7 gather_fusion.7
  24.0 0.7 gather_fusion.4
  24.7 0.6 gather_fusion.5
  25.4 0.7 iota_reduce_fusion.2
  26.1 0.7 iota_reduce_fusion
  26.8 0.6 pad.115.clone
  27.4 0.7 iota_reduce_fusion.3
  28.1 0.7 iota_reduce_fusion.1
  30.4 2.7 %collective-permute-start.1 = (f32[5,5,16,256]{3,2,1,0:T(8,128)S(1)}, f32[5,5,16,256]{3,2,1,0:T(8,128)S(1)}, u32[]{:S(2)}, u32[]{:S(2)}) collective-permute-start(f32[5,5,16,256]{3,2,1,0:T(8,128)S(1)} %broadcast_select_fusion.1), channel_id=1, source_target_pairs={{0,16},{8,24},{16,0},{24,8},{1,17},{9,25},{17,1},{25,9},{2,18},{10... | collective-permute-start | bytes 1228808 | tf_op jit(solution)/shard_map/ppermute | solution.py:15
  33.1 17.8 %collective-permute-done.1 = f32[5,5,16,256]{3,2,1,0:T(8,128)S(1)} collective-permute-done((f32[5,5,16,256]{3,2,1,0:T(8,128)S(1)}, f32[5,5,16,256]{3,2,1,0:T(8,128)S(1)}, u32[]{:S(2)}, u32[]{:S(2)}) %collective-permute-start.1) | collective-permute-done | bytes 409632 | tf_op jit(solution)/shard_map/ppermute | solution.py:15
  53.1 2.2 %collective-permute-start.3 = (f32[7,2,5,256]{3,1,2,0:T(2,128)S(1)}, f32[7,2,5,256]{3,1,2,0:T(2,128)S(1)}, u32[]{:S(2)}, u32[]{:S(2)}) collective-permute-start(f32[7,2,5,256]{3,1,2,0:T(2,128)S(1)} %pad_maximum_fusion.29), channel_id=1, source_target_pairs={{1,0},{2,1},{3,2},{4,3},{5,4},{6,5},{7,6},{0,7},{9,8},{10,9},{11,1... | collective-permute-start | bytes 215048 | tf_op jit(solution)/shard_map/ppermute | solution.py:21
  55.5 4.6 %collective-permute-done.2 = f32[7,2,5,256]{3,1,2,0:T(2,128)S(1)} collective-permute-done((f32[7,2,5,256]{3,1,2,0:T(2,128)S(1)}, f32[7,2,5,256]{3,1,2,0:T(2,128)S(1)}, u32[]{:S(2)}, u32[]{:S(2)}) %collective-permute-start.2) | collective-permute-done | bytes 71712 | tf_op jit(solution)/shard_map/ppermute | solution.py:21
  60.1 0.8 stack.25
  60.9 3.5 %all-to-all-start = ((f32[4,7,2,5,256]{4,2,3,1,0:T(2,128)}), f32[4,7,2,5,256]{4,2,3,1,0:T(2,128)S(1)}, u32[]{:S(2)}, u32[]{:S(2)}) async-start(f32[4,7,2,5,256]{4,2,3,1,0:T(2,128)} %stack.25), calls=%async_computation | async-start | bytes 573440 | tf_op jit(solution)/shard_map/all_to_all | solution.py:242
  64.9 15.9 %all_gather.9 = f32[28,2,5,256]{3,1,2,0:T(2,128)S(1)} all-gather(f32[7,2,5,256]{3,1,2,0:T(2,128)S(1)} %collective-permute-done.3), channel_id=1, replica_groups=mesh['row'=4,'col'=8] {'row'}, dimensions={0}, use_global_device_ids=true | all-gather | bytes 358400 | tf_op jit(solution)/shard_map/all_gather | solution.py:245
  83.6 1.6 %gather_fusion.6 = f32[7,5,256]{2,1,0:T(8,128)S(1)} fusion(f32[28,2,5,256]{3,2,1,0:T(8,128)} %bitcast.410, s32[7]{0:T(128)S(1)} %get-tuple-element.342), kind=kCustom, calls=%fused_computation.12 | custom fusion | bytes 71736 | tf_op jit(solution)/shard_map/gather | solution.py:247
  90.9 4.3 %collective-permute-done.4 = f32[7,2,5,256]{3,1,2,0:T(2,128)S(1)} collective-permute-done((f32[7,2,5,256]{3,1,2,0:T(2,128)S(1)}, f32[7,2,5,256]{3,1,2,0:T(2,128)S(1)}, u32[]{:S(2)}, u32[]{:S(2)}) %collective-permute-start.4) | collective-permute-done | bytes 71712 | tf_op jit(solution)/shard_map/ppermute | solution.py:21
  95.3 0.8 stack.56
  96.1 3.6 %all-to-all-start.1 = ((f32[4,7,2,5,256]{4,2,3,1,0:T(2,128)}), f32[4,7,2,5,256]{4,2,3,1,0:T(2,128)S(1)}, u32[]{:S(2)}, u32[]{:S(2)}) async-start(f32[4,7,2,5,256]{4,2,3,1,0:T(2,128)} %stack.56), calls=%async_computation.1 | async-start | bytes 573440 | tf_op jit(solution)/shard_map/all_to_all | solution.py:242
  100.2 15.6 %all_gather.10 = f32[28,2,5,256]{3,1,2,0:T(2,128)S(1)} all-gather(f32[7,2,5,256]{3,1,2,0:T(2,128)S(1)} %collective-permute-done.5), channel_id=1, replica_groups=mesh['row'=4,'col'=8] {'row'}, dimensions={0}, use_global_device_ids=true | all-gather | bytes 358400 | tf_op jit(solution)/shard_map/all_gather | solution.py:245
  124.7 4.2 %collective-permute-done.6 = f32[7,2,5,256]{3,1,2,0:T(2,128)S(1)} collective-permute-done((f32[7,2,5,256]{3,1,2,0:T(2,128)S(1)}, f32[7,2,5,256]{3,1,2,0:T(2,128)S(1)}, u32[]{:S(2)}, u32[]{:S(2)}) %collective-permute-start.6) | collective-permute-done | bytes 71712 | tf_op jit(solution)/shard_map/ppermute | solution.py:21
  128.9 0.8 stack.60
  129.7 3.5 %all-to-all-start.2 = ((f32[4,7,2,5,256]{4,2,3,1,0:T(2,128)}), f32[4,7,2,5,256]{4,2,3,1,0:T(2,128)S(1)}, u32[]{:S(2)}, u32[]{:S(2)}) async-start(f32[4,7,2,5,256]{4,2,3,1,0:T(2,128)} %stack.60), calls=%async_computation.2 | async-start | bytes 573440 | tf_op jit(solution)/shard_map/all_to_all | solution.py:242
  133.8 15.8 %all_gather.11 = f32[28,2,5,256]{3,1,2,0:T(2,128)S(1)} all-gather(f32[7,2,5,256]{3,1,2,0:T(2,128)S(1)} %collective-permute-done.7), channel_id=1, replica_groups=mesh['row'=4,'col'=8] {'row'}, dimensions={0}, use_global_device_ids=true | all-gather | bytes 358400 | tf_op jit(solution)/shard_map/all_gather | solution.py:245
  157.6 0.8 copy.181
  (295 shorter events, 35.0 us)
Async XLA Ops:
  9.4 19.5 %collective-permute-start = (f32[5,5,16,256]{3,2,1,0:T(8,128)S(1)}, f32[5,5,16,256]{3,2,1,0:T(8,128)S(1)}, u32[]{:S(2)}, u32[]{:S(2)}) collective-permute-start(f32[5,5,16,256]{3,2,1,0:T(8,128)S(1)} %broadcast_select_fusion.2), channel_id=1, source_target_pairs={{0,8},{8,0},{16,24},{24,16},{1,9},{9,1},{17,25},{25,17},{2,10},{10... | collective-permute-start | bytes 1228808 | tf_op jit(solution)/shard_map/ppermute | solution.py:15
  12.5 109.7 %copy-start.12 = (pred[256]{0:T(512)(128)(4,1)}, pred[256]{0:T(512)(128)(4,1)S(1)}, u32[]{:S(2)}) copy-start(pred[256]{0:T(512)(128)(4,1)S(1)} %get-tuple-element.346) | copy-start | bytes 772
  12.5 109.7 %copy-start.14 = (pred[256]{0:T(512)(128)(4,1)}, pred[256]{0:T(512)(128)(4,1)S(1)}, u32[]{:S(2)}) copy-start(pred[256]{0:T(512)(128)(4,1)S(1)} %get-tuple-element.347) | copy-start | bytes 772
  22.5 6.3 %copy-start = (f32[11,5,16,256]{3,2,1,0:T(8,128)S(1)}, f32[11,5,16,256]{3,2,1,0:T(8,128)}, u32[]{:S(2)}) copy-start(f32[11,5,16,256]{3,2,1,0:T(8,128)} %param.45) | copy-start | bytes 2703364
  22.7 28.9 %copy-start.10 = (pred[7]{0:T(512)(128)(4,1)}, pred[7]{0:T(512)(128)(4,1)S(1)}, u32[]{:S(2)}) copy-start(pred[7]{0:T(512)(128)(4,1)S(1)} %compare_bitcast_fusion) | copy-start | bytes 25
  30.4 20.5 %collective-permute-start.1 = (f32[5,5,16,256]{3,2,1,0:T(8,128)S(1)}, f32[5,5,16,256]{3,2,1,0:T(8,128)S(1)}, u32[]{:S(2)}, u32[]{:S(2)}) collective-permute-start(f32[5,5,16,256]{3,2,1,0:T(8,128)S(1)} %broadcast_select_fusion.1), channel_id=1, source_target_pairs={{0,16},{8,24},{16,0},{24,8},{1,17},{9,25},{17,1},{25,9},{2,18},{10... | collective-permute-start | bytes 1228808 | tf_op jit(solution)/shard_map/ppermute | solution.py:15
  33.0 82.8 %copy-start.8 = (s32[7]{0:T(128)}, s32[7]{0:T(128)S(1)}, u32[]{:S(2)}) copy-start(s32[7]{0:T(128)S(1)} %get-tuple-element.345) | copy-start | bytes 88
  33.0 83.4 %copy-start.6 = (s32[7]{0:T(128)}, s32[7]{0:T(128)S(1)}, u32[]{:S(2)}) copy-start(s32[7]{0:T(128)S(1)} %get-tuple-element.344) | copy-start | bytes 88
  33.1 84.3 %copy-start.4 = (s32[7]{0:T(128)}, s32[7]{0:T(128)S(1)}, u32[]{:S(2)}) copy-start(s32[7]{0:T(128)S(1)} %get-tuple-element.343) | copy-start | bytes 88
  33.1 84.9 %copy-start.2 = (s32[7]{0:T(128)}, s32[7]{0:T(128)S(1)}, u32[]{:S(2)}) copy-start(s32[7]{0:T(128)S(1)} %get-tuple-element.342) | copy-start | bytes 88
  51.0 0.7 copy-start.18
  53.1 11.7 %collective-permute-start.3 = (f32[7,2,5,256]{3,1,2,0:T(2,128)S(1)}, f32[7,2,5,256]{3,1,2,0:T(2,128)S(1)}, u32[]{:S(2)}, u32[]{:S(2)}) collective-permute-start(f32[7,2,5,256]{3,1,2,0:T(2,128)S(1)} %pad_maximum_fusion.29), channel_id=1, source_target_pairs={{1,0},{2,1},{3,2},{4,3},{5,4},{6,5},{7,6},{0,7},{9,8},{10,9},{11,1... | collective-permute-start | bytes 215048 | tf_op jit(solution)/shard_map/ppermute | solution.py:21
  55.4 4.7 %collective-permute-start.2 = (f32[7,2,5,256]{3,1,2,0:T(2,128)S(1)}, f32[7,2,5,256]{3,1,2,0:T(2,128)S(1)}, u32[]{:S(2)}, u32[]{:S(2)}) collective-permute-start(f32[7,2,5,256]{3,1,2,0:T(2,128)S(1)} %pad_maximum_fusion.28), channel_id=1, source_target_pairs={{7,0},{0,1},{1,2},{2,3},{3,4},{4,5},{5,6},{6,7},{15,8},{8,9},{9,10... | collective-permute-start | bytes 215048 | tf_op jit(solution)/shard_map/ppermute | solution.py:21
  60.9 21.4 %all-to-all-start = ((f32[4,7,2,5,256]{4,2,3,1,0:T(2,128)}), f32[4,7,2,5,256]{4,2,3,1,0:T(2,128)S(1)}, u32[]{:S(2)}, u32[]{:S(2)}) async-start(f32[4,7,2,5,256]{4,2,3,1,0:T(2,128)} %stack.25), calls=%async_computation | async-start | bytes 573440 | tf_op jit(solution)/shard_map/all_to_all | solution.py:242
  82.3 0.8 copy-start.1
  87.8 0.7 copy-start.16
  90.2 10.0 %collective-permute-start.5 = (f32[7,2,5,256]{3,1,2,0:T(2,128)S(1)}, f32[7,2,5,256]{3,1,2,0:T(2,128)S(1)}, u32[]{:S(2)}, u32[]{:S(2)}) collective-permute-start(f32[7,2,5,256]{3,1,2,0:T(2,128)S(1)} %pad_maximum_fusion.31), channel_id=1, source_target_pairs={{1,0},{2,1},{3,2},{4,3},{5,4},{6,5},{7,6},{0,7},{9,8},{10,9},{11,1... | collective-permute-start | bytes 215048 | tf_op jit(solution)/shard_map/ppermute | solution.py:21
  90.3 4.9 %collective-permute-start.4 = (f32[7,2,5,256]{3,1,2,0:T(2,128)S(1)}, f32[7,2,5,256]{3,1,2,0:T(2,128)S(1)}, u32[]{:S(2)}, u32[]{:S(2)}) collective-permute-start(f32[7,2,5,256]{3,1,2,0:T(2,128)S(1)} %pad_maximum_fusion.30), channel_id=1, source_target_pairs={{7,0},{0,1},{1,2},{2,3},{3,4},{4,5},{5,6},{6,7},{15,8},{8,9},{9,10... | collective-permute-start | bytes 215048 | tf_op jit(solution)/shard_map/ppermute | solution.py:21
  96.1 21.2 %all-to-all-start.1 = ((f32[4,7,2,5,256]{4,2,3,1,0:T(2,128)}), f32[4,7,2,5,256]{4,2,3,1,0:T(2,128)S(1)}, u32[]{:S(2)}, u32[]{:S(2)}) async-start(f32[4,7,2,5,256]{4,2,3,1,0:T(2,128)} %stack.56), calls=%async_computation.1 | async-start | bytes 573440 | tf_op jit(solution)/shard_map/all_to_all | solution.py:242
  124.0 9.8 %collective-permute-start.7 = (f32[7,2,5,256]{3,1,2,0:T(2,128)S(1)}, f32[7,2,5,256]{3,1,2,0:T(2,128)S(1)}, u32[]{:S(2)}, u32[]{:S(2)}) collective-permute-start(f32[7,2,5,256]{3,1,2,0:T(2,128)S(1)} %pad_maximum_fusion.33), channel_id=1, source_target_pairs={{1,0},{2,1},{3,2},{4,3},{5,4},{6,5},{7,6},{0,7},{9,8},{10,9},{11,1... | collective-permute-start | bytes 215048 | tf_op jit(solution)/shard_map/ppermute | solution.py:21
  124.1 4.8 %collective-permute-start.6 = (f32[7,2,5,256]{3,1,2,0:T(2,128)S(1)}, f32[7,2,5,256]{3,1,2,0:T(2,128)S(1)}, u32[]{:S(2)}, u32[]{:S(2)}) collective-permute-start(f32[7,2,5,256]{3,1,2,0:T(2,128)S(1)} %pad_maximum_fusion.32), channel_id=1, source_target_pairs={{7,0},{0,1},{1,2},{2,3},{3,4},{4,5},{5,6},{6,7},{15,8},{8,9},{9,10... | collective-permute-start | bytes 215048 | tf_op jit(solution)/shard_map/ppermute | solution.py:21
  129.7 21.3 %all-to-all-start.2 = ((f32[4,7,2,5,256]{4,2,3,1,0:T(2,128)}), f32[4,7,2,5,256]{4,2,3,1,0:T(2,128)S(1)}, u32[]{:S(2)}, u32[]{:S(2)}) async-start(f32[4,7,2,5,256]{4,2,3,1,0:T(2,128)} %stack.60), calls=%async_computation.2 | async-start | bytes 573440 | tf_op jit(solution)/shard_map/all_to_all | solution.py:242
  133.6 16.1 %copy-start.9 = (s32[7]{0:T(128)S(1)}, s32[7]{0:T(128)}, u32[]{:S(2)}) copy-start(s32[7]{0:T(128)} %copy-done.8) | copy-start | bytes 88
  133.6 16.7 %copy-start.7 = (s32[7]{0:T(128)S(1)}, s32[7]{0:T(128)}, u32[]{:S(2)}) copy-start(s32[7]{0:T(128)} %copy-done.6) | copy-start | bytes 88
  133.7 17.4 %copy-start.5 = (s32[7]{0:T(128)S(1)}, s32[7]{0:T(128)}, u32[]{:S(2)}) copy-start(s32[7]{0:T(128)} %copy-done.4) | copy-start | bytes 88
  133.7 18.0 %copy-start.3 = (s32[7]{0:T(128)S(1)}, s32[7]{0:T(128)}, u32[]{:S(2)}) copy-start(s32[7]{0:T(128)} %copy-done.2) | copy-start | bytes 88
  155.6 0.7 copy-start.13
  155.6 0.7 copy-start.15
  155.6 0.7 copy-start.17
  156.8 0.6 copy-start.11
